TPU v7x, 32 devices: a whole 2x2x4 slice. The times are simulated.
32 devices in a mesh: dom: 16 (over z, x, core), band: 2 (over y).
Axes of the slice: x: 2, y: 2, z: 4, core: 2. Of those that a mesh axis runs over, the one named last changes fastest.
Arguments:
- wavefun: float32 [13824, 512], P('dom', 'band')
- cell_ops: float32 [64, 343, 343], P('dom'), as said below
- cell_map: int32 [64, 343], P('dom'), may hold values from 0 to 1007, as said below
- face_list: int32 [2304], P('dom'), may hold values from 0 to 863, as said below
Outputs:
- ortho_bands: float32 [13824, 512], P('dom', 'band')
Inputs may be any that keep to these rules, and one draw needn't show every extreme that they name: `cell_map`: each row lists the 343 distinct local numbers of a cell's nodes; a number below 864 is a node of the cell's own domain, 864 + j stands for the j-th lower face node of the next domain (periodic over domains); every node of a domain belongs to some cell of that domain. `face_list`: the 144 entries of each domain are distinct node numbers of that domain. `cell_ops`: each cell's matrix is symmetric.
All inputs are finite; a program needn't handle non-finite values.
Results may differ from a plain program's by a relative error of at most 0.0001.
Values sent between devices are 32-bit elements; how exact they have to be, the bound alone decides.
A program may use at most 64 MiB of HBM per device.

v0:
```python
import jax
import jax.numpy as jnp
from jax import lax
from jax.sharding import PartitionSpec as P

DEGREE = 2
cheb_centre = 1.0
cheb_half = 1.6


def shifted(block, axis, distance):
    devices = range(lax.axis_size(axis))
    route = [((i - distance) % len(devices), i) for i in devices]
    return lax.ppermute(block, axis, route)


def on_device(wavefun, cell_ops, cell_map, face_list):
    owned_rows = wavefun.shape[0]
    block_width = wavefun.shape[1]
    flat_map = cell_map.reshape(-1)

    def local_apply(extended):
        cell_values = extended[flat_map].reshape(cell_map.shape[0], cell_map.shape[1], block_width)
        products = jnp.einsum(
            "cij,cjb->cib", cell_ops, cell_values, precision=lax.Precision.HIGHEST
        )
        return jnp.zeros_like(extended).at[flat_map].add(products.reshape(-1, block_width))

    def operate(vector):
        fetched = shifted(vector[face_list], "dom", -1)
        applied = local_apply(jnp.concatenate([vector, fetched], 0))
        returned = shifted(applied[owned_rows:], "dom", 1)
        return applied[:owned_rows].at[face_list].add(returned)

    latest = (operate(wavefun) - cheb_centre * wavefun) / cheb_half

    def advance(counter, carried):
        earlier, current = carried
        following = 2.0 * (operate(current) - cheb_centre * current) / cheb_half - earlier
        return (current, following)

    earlier, latest = lax.fori_loop(1, DEGREE, advance, (wavefun, latest))
    full_bands = lax.all_gather(latest, "band", axis=1, tiled=True)
    partial_value = jnp.einsum("nb,nc->bc", full_bands, full_bands, precision=lax.Precision.HIGHEST)
    margin = lax.psum(partial_value, "dom")
    norm_value = jnp.sqrt(jnp.sum(margin * margin) + 1e-06)
    full_width = margin.shape[0]
    offset = lax.axis_index("band") * block_width
    scaled_cols = lax.dynamic_slice_in_dim(margin, offset, block_width, 1) / norm_value
    identity_cols = lax.dynamic_slice_in_dim(
        jnp.eye(full_width, dtype=jnp.float32), offset, block_width, 1
    )
    mixing = (3.0 * identity_cols - scaled_cols) / 2.0
    return jnp.dot(full_bands, mixing, precision=lax.Precision.HIGHEST)


def solution(mesh):
    return jax.shard_map(
        on_device,
        mesh=mesh,
        in_specs=(P("dom", "band"), P("dom", None, None), P("dom", None), P("dom")),
        out_specs=P("dom", "band"),
        check_vma=False,
    )
```

profile of v0, /device:TPU:0, one launch (start us, length us, event | category | flops | bytes accessed | tf_op | source)
XLA Modules:
  0.0 234.2 jit_solution(618638592340945098)
XLA Ops:
  6.5 0.0 copy-start
  6.5 0.0 all-gather.2.cloned.1.call-start
  6.5 0.8 compare_select_fusion.1
  7.4 2.0 gather_fusion
  9.3 5.5 %collective-permute-start = (f32[144,256]{1,0:T(8,128)S(1)}, f32[144,256]{1,0:T(8,128)S(1)}, u32[]{:S(2)}, u32[]{:S(2)}) collective-permute-start(f32[144,256]{1,0:T(8,128)S(1)} %gather_fusion), channel_id=1, source_target_pairs={{2,0},{4,2},{6,4},{8,6},{10,8},{12,10},{14,12},{16,14},{18,16},{20... | collective-permute-start | bytes 442376 | tf_op jit(solution)/shard_map/ppermute | solution.py:14
  14.8 0.8 reshape.45
  15.7 1.9 collective-permute-done
  17.5 1.2 pad_maximum_fusion
  18.7 4.6 %gather_fusion.1 = f32[1372,256]{1,0:T(8,128)} fusion(f32[1008,256]{1,0:T(8,128)S(1)} %pad_maximum_fusion, s32[2048]{0:T(1024)S(1)} %pad_clamp_fusion), kind=kCustom, calls=%fused_computation.1 | custom fusion | bytes 2815344 | tf_op jit(solution)/shard_map/gather | solution.py:23
  23.3 1.5 reshape.46
  24.8 0.0 copy-done
  24.8 3.7 %fusion.4 = f32[4,343,256]{2,1,0:T(8,128)} fusion(f32[4,343,256]{2,1,0:T(8,128)S(1)} %reshape.46, f32[4,343,343]{2,0,1:T(4,128)S(1)} %copy-done), kind=kOutput, calls=%fused_computation.12 | convolution fusion | flops 1445670912 | bytes 4692240 | tf_op jit(solution)/shard_map/cij,cjb->cib/dot_general | solution.py:24
  28.5 2.6 %reshape.86 = f32[1372,256]{1,0:T(8,128)} reshape(f32[4,343,256]{2,1,0:T(8,128)} %fusion.4) | data formatting | bytes 2809856 | tf_op jit(solution)/shard_map/reshape | solution.py:27
  31.1 8.7 %scatter_custom_fusion = f32[1008,256]{1,0:T(8,128)S(1)} fusion(s32[1372]{0:T(1024)S(1)} %fusion.25, f32[1372,256]{1,0:T(8,128)} %reshape.86, f32[]{:T(128)} %constant.12.clone.1), kind=kCustom, calls=%fused_computation.29 | custom fusion | flops 351232 | bytes 1032704 | tf_op jit(solution)/shard_map/scatter-add | solution.py:27
  39.9 0.0 copy-start.3
  39.9 1.0 copy-done.3
  40.8 0.0 collective-permute-start.1
  40.9 1.2 slice.26
  42.1 6.2 %collective-permute-done.1 = f32[144,256]{1,0:T(8,128)S(1)} collective-permute-done((f32[144,256]{1,0:T(8,128)S(1)}, f32[144,256]{1,0:T(8,128)S(1)}, u32[]{:S(2)}, u32[]{:S(2)}) %collective-permute-start.1) | collective-permute-done | bytes 147488 | tf_op jit(solution)/shard_map/ppermute | solution.py:14
  48.3 1.7 scatter_fusion
  50.0 0.0 copy-start.1
  50.0 2.6 %subtract_multiply_fusion = f32[864,256]{1,0:T(8,128)} fusion(f32[864,256]{1,0:T(8,128)S(1)} %scatter_fusion, f32[864,256]{1,0:T(8,128)} %param.4), kind=kLoop, calls=%fused_computation.18 | loop fusion | flops 442368 | bytes 2654208 | tf_op jit(solution)/shard_map/div | solution.py:35
  52.5 2.0 gather_fusion.2
  54.5 0.0 copy-done.1
  54.5 0.2 collective-permute-start.2
  54.8 2.7 %collective-permute-done.2 = f32[144,256]{1,0:T(8,128)S(1)} collective-permute-done((f32[144,256]{1,0:T(8,128)S(1)}, f32[144,256]{1,0:T(8,128)S(1)}, u32[]{:S(2)}, u32[]{:S(2)}) %collective-permute-start.2) | collective-permute-done | bytes 147488 | tf_op jit(solution)/shard_map/while/body/eval_jaxpr/ppermute | solution.py:14
  57.4 1.2 pad_maximum_fusion.1
  58.7 4.6 %gather_fusion.3 = f32[1372,256]{1,0:T(8,128)} fusion(f32[1008,256]{1,0:T(8,128)S(1)} %pad_maximum_fusion.1, s32[2048]{0:T(1024)S(1)} %pad_clamp_fusion), kind=kCustom, calls=%fused_computation.3 | custom fusion | bytes 2815344 | tf_op jit(solution)/shard_map/while/body/eval_jaxpr/gather | solution.py:23
  63.2 1.5 reshape.48
  64.7 3.7 %fusion.7 = f32[4,343,256]{2,1,0:T(8,128)} fusion(f32[4,343,256]{2,1,0:T(8,128)S(1)} %reshape.48, f32[4,343,343]{2,0,1:T(4,128)S(1)} %copy-done), kind=kOutput, calls=%fused_computation.13 | convolution fusion | flops 1445670912 | bytes 4692240 | tf_op jit(solution)/shard_map/while/body/eval_jaxpr/cij,cjb->cib/dot_general | solution.py:24
  68.4 2.6 %reshape.102 = f32[1372,256]{1,0:T(8,128)} reshape(f32[4,343,256]{2,1,0:T(8,128)} %fusion.7) | data formatting | bytes 2809856 | tf_op jit(solution)/shard_map/while/body/eval_jaxpr/reshape | solution.py:27
  71.0 8.7 %scatter_custom_fusion.2 = f32[1008,256]{1,0:T(8,128)S(1)} fusion(s32[1372]{0:T(1024)S(1)} %fusion.25, f32[1372,256]{1,0:T(8,128)} %reshape.102, f32[]{:T(128)} %constant.12.clone.1), kind=kCustom, calls=%fused_computation.27 | custom fusion | flops 351232 | bytes 1032704 | tf_op jit(solution)/shard_map/while/body/eval_jaxpr/scatter-add | solution.py:27
  79.8 0.1 collective-permute-start.3
  79.8 1.0 slice.28
  80.8 0.0 copy-start.2
  80.8 6.4 %collective-permute-done.3 = f32[144,256]{1,0:T(8,128)S(1)} collective-permute-done((f32[144,256]{1,0:T(8,128)S(1)}, f32[144,256]{1,0:T(8,128)S(1)}, u32[]{:S(2)}, u32[]{:S(2)}) %collective-permute-start.3) | collective-permute-done | bytes 147488 | tf_op jit(solution)/shard_map/while/body/eval_jaxpr/ppermute | solution.py:14
  87.3 3.3 %scatter_fusion.1 = f32[864,256]{1,0:T(8,128)} fusion(f32[864,256]{1,0:T(8,128)} %slice.28, s32[144]{0:T(256)S(1)} %compare_select_fusion.1, f32[144,256]{1,0:T(8,128)S(1)} %collective-permute-done.3), kind=kCustom, calls=%fused_computation.7 | custom fusion | flops 36864 | bytes 442944 | tf_op jit(solution)/shard_map/while/body/eval_jaxpr/scatter-add | solution.py:33
  90.6 0.0 copy-done.2
  90.6 2.6 %multiply_subtract_fusion = f32[864,256]{1,0:T(8,128)} fusion(f32[864,256]{1,0:T(8,128)} %param.4, f32[864,256]{1,0:T(8,128)} %scatter_fusion.1, f32[864,256]{1,0:T(8,128)S(1)} %copy-done.2), kind=kLoop, calls=%fused_computation.17 | loop fusion | flops 1105920 | bytes 3538944 | tf_op jit(solution)/shard_map/while/body/eval_jaxpr/sub | solution.py:39
  93.2 0.0 all-gather.2.cloned.1.call-update
  93.2 0.3 all-reduce.2.cloned.1.call-start
  93.5 26.6 %all-gather.2.cloned.1.call-done = f32[864,512]{1,0:T(8,128)} async-done(((f32[864,256]{1,0:T(8,128)}), f32[864,512]{1,0:T(8,128)}) %all-gather.2.cloned.1.call-update) | async-done | bytes 1769488 | tf_op jit(solution)/shard_map/all_gather | solution.py:43
  120.0 6.5 %fusion.29 = f32[512,512]{1,0:T(8,128)} fusion(f32[864,512]{1,0:T(8,128)} %all-gather.2.cloned.1.call-done), kind=kOutput, calls=%fused_computation.43 | convolution fusion | flops 2717908992 | bytes 2818048 | tf_op jit(solution)/shard_map/nb,nc->bc/dot_general | solution.py:44
  126.6 0.0 all-reduce.2.cloned.1.call-update
  126.6 93.8 %all-reduce.2.cloned.1.call-done = f32[512,512]{1,0:T(8,128)} async-done(((f32[512,512]{1,0:T(8,128)}), f32[512,512]{1,0:T(8,128)}) %all-reduce.2.cloned.1.call-update) | async-done | bytes 1048592 | tf_op jit(solution)/shard_map/psum | solution.py:45
  220.5 2.1 multiply_reduce_fusion
  223.2 4.1 %fusion.10 = f32[864,256]{1,0:T(8,128)} fusion(f32[864,512]{1,0:T(8,128)} %all-gather.2.cloned.1.call-done, f32[512,512]{1,0:T(8,128)} %all-reduce.2.cloned.1.call-done, s32[]{:T(128)S(6)} %select_n.27, f32[]{:T(128)S(6)} %sqrt.3), kind=kOutput, calls=%fused_computation.20 | convolution fusion | flops 1359872000 | bytes 3180032 | tf_op jit(solution)/shard_map/dot_general | solution.py:54
  (5 shorter events, 0.1 us)
Async XLA Ops:
  6.5 18.3 %copy-start = (f32[4,343,343]{2,0,1:T(4,128)S(1)}, f32[4,343,343]{2,0,1:T(4,128)}, u32[]{:S(2)}) copy-start(f32[4,343,343]{2,0,1:T(4,128)} %param.5) | copy-start | bytes 5647156
  6.5 113.5 %all-gather.2.cloned.1.call-start = ((), (), s32[]{:S(2)}) async-start(), calls=%async_computation | async-start | bytes 2654208 | tf_op jit(solution)/shard_map/all_gather | solution.py:43
  9.3 8.2 %collective-permute-start = (f32[144,256]{1,0:T(8,128)S(1)}, f32[144,256]{1,0:T(8,128)S(1)}, u32[]{:S(2)}, u32[]{:S(2)}) collective-permute-start(f32[144,256]{1,0:T(8,128)S(1)} %gather_fusion), channel_id=1, source_target_pairs={{2,0},{4,2},{6,4},{8,6},{10,8},{12,10},{14,12},{16,14},{18,16},{20... | collective-permute-start | bytes 442376 | tf_op jit(solution)/shard_map/ppermute | solution.py:14
  39.9 1.0 copy-start.3
  40.8 7.4 %collective-permute-start.1 = (f32[144,256]{1,0:T(8,128)S(1)}, f32[144,256]{1,0:T(8,128)S(1)}, u32[]{:S(2)}, u32[]{:S(2)}) collective-permute-start(f32[144,256]{1,0:T(8,128)S(1)} %slice.27), channel_id=1, source_target_pairs={{30,0},{0,2},{2,4},{4,6},{6,8},{8,10},{10,12},{12,14},{14,16},{16,... | collective-permute-start | bytes 442376 | tf_op jit(solution)/shard_map/ppermute | solution.py:14
  50.0 4.5 %copy-start.1 = (f32[864,256]{1,0:T(8,128)}, f32[864,256]{1,0:T(8,128)S(1)}, u32[]{:S(2)}) copy-start(f32[864,256]{1,0:T(8,128)S(1)} %scatter_fusion) | copy-start | bytes 2654212
  54.5 2.9 %collective-permute-start.2 = (f32[144,256]{1,0:T(8,128)S(1)}, f32[144,256]{1,0:T(8,128)S(1)}, u32[]{:S(2)}, u32[]{:S(2)}) collective-permute-start(f32[144,256]{1,0:T(8,128)S(1)} %gather_fusion.2), channel_id=1, source_target_pairs={{2,0},{4,2},{6,4},{8,6},{10,8},{12,10},{14,12},{16,14},{18,16},{20... | collective-permute-start | bytes 442376 | tf_op jit(solution)/shard_map/while/body/eval_jaxpr/ppermute | solution.py:14
  79.8 7.5 %collective-permute-start.3 = (f32[144,256]{1,0:T(8,128)S(1)}, f32[144,256]{1,0:T(8,128)S(1)}, u32[]{:S(2)}, u32[]{:S(2)}) collective-permute-start(f32[144,256]{1,0:T(8,128)S(1)} %slice.29), channel_id=1, source_target_pairs={{30,0},{0,2},{2,4},{4,6},{6,8},{8,10},{10,12},{12,14},{14,16},{16,... | collective-permute-start | bytes 442376 | tf_op jit(solution)/shard_map/while/body/eval_jaxpr/ppermute | solution.py:14
  80.8 9.8 %copy-start.2 = (f32[864,256]{1,0:T(8,128)S(1)}, f32[864,256]{1,0:T(8,128)}, u32[]{:S(2)}) copy-start(f32[864,256]{1,0:T(8,128)} %copy-done.1) | copy-start | bytes 2654212
  93.2 127.3 %all-reduce.2.cloned.1.call-start = ((), (), s32[]{:S(2)}) async-start(), calls=%async_computation.1 | async-start | bytes 2097152 | tf_op jit(solution)/shard_map/psum | solution.py:45
Sparse Core Ops, SparseCore 0:
  93.3 26.6 all-gather.1
  126.7 93.6 all-reduce.1
where the time goes:
time: 235 us; the launch traced here: 234 us
  waiting for transfers between devices  138 us (59%)
  other arithmetic  33.1 us (14%)
  local copies, waits for them, and re-layouts  25.3 us (11%)
  matrix products  18 us (8%)
  between operations  14.2 us (6%)
  starting transfers between devices  6.06 us (3%)
    psum x1, waiting for transfers between devices, on_device(): margin = lax.psum(partial_value, 'dom')  93.8 us
    all_gather x1, waiting for transfers between devices, on_device(): full_bands = lax.all_gather(latest, 'band', axis=1, tiled=True)  26.6 us
    scatter-add x2, other arithmetic, local_apply(): jnp.zeros_like(extended).at[flat_map].add(products.reshape(-1, block_width))  17.4 us
    ppermute x4, waiting for transfers between devices, shifted(): return lax.ppermute(block, axis, route)  17.1 us
    gather x2, local copies, waits for them, and re-layouts, local_apply(): extended[flat_map]  9.14 us
    dot_general x2, matrix products, local_apply(): jnp.einsum('cij,cjb->cib', cell_ops, cell_values, precision=lax.Precision...  7.36 us
    dot_general x1, matrix products, on_device(): jnp.einsum('nb,nc->bc', full_bands, full_bands, precision=lax.Precision.H...  6.54 us
    ppermute x4, starting transfers between devices, shifted(): return lax.ppermute(block, axis, route)  5.8 us
  transfers between devices with their start and end apart: 6, of which 6 were waited for; matrix products, arithmetic and copies ran while one was open for 1% of the time, Pallas kernels for 0%

commit v1 on v0

--- a/solution.py
+++ b/solution.py
@@ -6,6 +6,18 @@
 DEGREE = 2
 cheb_centre = 1.0
 cheb_half = 1.6
+
+
+def collect(value, axis, dim):
+    ways, here, turn = (lax.axis_size(axis), lax.axis_index(axis), value.shape[dim])
+    line, have = (value, 1)
+    while have < ways:
+        line = jnp.concatenate(
+            [line, lax.ppermute(line, axis, [(d, (d - have) % ways) for d in range(ways)])],
+            axis=dim,
+        )
+        have = 2 * have
+    return jnp.roll(line, here * turn, axis=dim)
 
 
 def shifted(block, axis, distance):
@@ -40,7 +52,7 @@
         return (current, following)
 
     earlier, latest = lax.fori_loop(1, DEGREE, advance, (wavefun, latest))
-    full_bands = lax.all_gather(latest, "band", axis=1, tiled=True)
+    full_bands = collect(latest, "band", 1)
     partial_value = jnp.einsum("nb,nc->bc", full_bands, full_bands, precision=lax.Precision.HIGHEST)
     margin = lax.psum(partial_value, "dom")
     norm_value = jnp.sqrt(jnp.sum(margin * margin) + 1e-06)

time: 235 us -> 227 us (0.966)
  waiting for transfers between devices: 138 us -> 128 us
    all_gather x1 -> x0, waiting for transfers between devices: 26.6 us -> none  [on_device(): full_bands = lax.all_gather(latest, 'band', axis=1, tiled=True)]
    ppermute x0 -> x1, waiting for transfers between devices: none -> 14.2 us  [collect(): lax.ppermute(line, axis, [(d, (d - have) % ways) for d in range(ways)])]
    psum x1, waiting for transfers between devices: 93.8 us -> 96.2 us  [on_device(): margin = lax.psum(partial_value, 'dom')]
where the time goes in v1:
time: 227 us; the launch traced here: 226 us
  waiting for transfers between devices  128 us (56%)
  other arithmetic  34.6 us (15%)
  local copies, waits for them, and re-layouts  26.5 us (12%)
  matrix products  16 us (7%)
  between operations  14.2 us (6%)
  starting transfers between devices  7.32 us (3%)
    psum x1, waiting for transfers between devices, on_device(): margin = lax.psum(partial_value, 'dom')  96.2 us
    scatter-add x2, other arithmetic, local_apply(): jnp.zeros_like(extended).at[flat_map].add(products.reshape(-1, block_width))  17.4 us
    ppermute x4, waiting for transfers between devices, shifted(): return lax.ppermute(block, axis, route)  17.1 us
    ppermute x1, waiting for transfers between devices, collect(): lax.ppermute(line, axis, [(d, (d - have) % ways) for d in range(ways)])  14.2 us
    gather x2, local copies, waits for them, and re-layouts, local_apply(): extended[flat_map]  9.14 us
    dot_general x2, matrix products, local_apply(): jnp.einsum('cij,cjb->cib', cell_ops, cell_values, precision=lax.Precision...  7.36 us
    ppermute x4, starting transfers between devices, shifted(): return lax.ppermute(block, axis, route)  5.8 us
    reshape x2, local copies, waits for them, and re-layouts, local_apply(): products.reshape(-1, block_width)  5.23 us
  transfers between devices with their start and end apart: 6, of which 6 were waited for; matrix products, arithmetic and copies ran while one was open for 1% of the time, Pallas kernels for 0%

profile of v1, /device:TPU:0, one launch (start us, length us, event | category | flops | bytes accessed | tf_op | source)
XLA Modules:
  0.0 226.2 jit_solution(11402799181223061827)
XLA Ops:
  6.5 0.0 copy-start
  6.5 0.0 all-reduce.2.cloned.1.call-start
  6.5 0.8 compare_select_fusion.1
  7.4 2.0 gather_fusion
  9.3 5.5 %collective-permute-start = (f32[144,256]{1,0:T(8,128)S(1)}, f32[144,256]{1,0:T(8,128)S(1)}, u32[]{:S(2)}, u32[]{:S(2)}) collective-permute-start(f32[144,256]{1,0:T(8,128)S(1)} %gather_fusion), channel_id=1, source_target_pairs={{2,0},{4,2},{6,4},{8,6},{10,8},{12,10},{14,12},{16,14},{18,16},{20... | collective-permute-start | bytes 442376 | tf_op jit(solution)/shard_map/ppermute | solution.py:26
  14.8 0.8 reshape.45
  15.7 1.9 collective-permute-done
  17.5 1.2 pad_maximum_fusion
  18.7 4.6 %gather_fusion.1 = f32[1372,256]{1,0:T(8,128)} fusion(f32[1008,256]{1,0:T(8,128)S(1)} %pad_maximum_fusion, s32[2048]{0:T(1024)S(1)} %pad_clamp_fusion), kind=kCustom, calls=%fused_computation.1 | custom fusion | bytes 2815344 | tf_op jit(solution)/shard_map/gather | solution.py:35
  23.3 1.5 reshape.46
  24.8 0.0 copy-done
  24.8 3.7 %fusion.7 = f32[4,343,256]{2,1,0:T(8,128)} fusion(f32[4,343,256]{2,1,0:T(8,128)S(1)} %reshape.46, f32[4,343,343]{2,0,1:T(4,128)S(1)} %copy-done), kind=kOutput, calls=%fused_computation.19 | convolution fusion | flops 1445670912 | bytes 4692240 | tf_op jit(solution)/shard_map/cij,cjb->cib/dot_general | solution.py:36
  28.5 2.6 %reshape.86 = f32[1372,256]{1,0:T(8,128)} reshape(f32[4,343,256]{2,1,0:T(8,128)} %fusion.7) | data formatting | bytes 2809856 | tf_op jit(solution)/shard_map/reshape | solution.py:39
  31.1 8.7 %scatter_custom_fusion = f32[1008,256]{1,0:T(8,128)S(1)} fusion(s32[1372]{0:T(1024)S(1)} %fusion.28, f32[1372,256]{1,0:T(8,128)} %reshape.86, f32[]{:T(128)} %constant.34.clone.1), kind=kCustom, calls=%fused_computation.36 | custom fusion | flops 351232 | bytes 1032704 | tf_op jit(solution)/shard_map/scatter-add | solution.py:39
  39.9 0.0 copy-start.4
  39.9 1.0 copy-done.4
  40.8 0.0 collective-permute-start.1
  40.9 1.2 slice.26
  42.1 6.2 %collective-permute-done.1 = f32[144,256]{1,0:T(8,128)S(1)} collective-permute-done((f32[144,256]{1,0:T(8,128)S(1)}, f32[144,256]{1,0:T(8,128)S(1)}, u32[]{:S(2)}, u32[]{:S(2)}) %collective-permute-start.1) | collective-permute-done | bytes 147488 | tf_op jit(solution)/shard_map/ppermute | solution.py:26
  48.3 1.7 scatter_fusion
  50.0 0.0 copy-start.2
  50.0 2.6 %subtract_multiply_fusion = f32[864,256]{1,0:T(8,128)} fusion(f32[864,256]{1,0:T(8,128)S(1)} %scatter_fusion, f32[864,256]{1,0:T(8,128)} %param.4), kind=kLoop, calls=%fused_computation.25 | loop fusion | flops 442368 | bytes 2654208 | tf_op jit(solution)/shard_map/div | solution.py:47
  52.5 2.0 gather_fusion.2
  54.5 0.0 copy-done.2
  54.5 0.2 collective-permute-start.2
  54.8 2.7 %collective-permute-done.2 = f32[144,256]{1,0:T(8,128)S(1)} collective-permute-done((f32[144,256]{1,0:T(8,128)S(1)}, f32[144,256]{1,0:T(8,128)S(1)}, u32[]{:S(2)}, u32[]{:S(2)}) %collective-permute-start.2) | collective-permute-done | bytes 147488 | tf_op jit(solution)/shard_map/while/body/eval_jaxpr/ppermute | solution.py:26
  57.4 1.2 pad_maximum_fusion.1
  58.7 4.6 %gather_fusion.3 = f32[1372,256]{1,0:T(8,128)} fusion(f32[1008,256]{1,0:T(8,128)S(1)} %pad_maximum_fusion.1, s32[2048]{0:T(1024)S(1)} %pad_clamp_fusion), kind=kCustom, calls=%fused_computation.3 | custom fusion | bytes 2815344 | tf_op jit(solution)/shard_map/while/body/eval_jaxpr/gather | solution.py:35
  63.2 1.5 reshape.48
  64.7 3.7 %fusion.10 = f32[4,343,256]{2,1,0:T(8,128)} fusion(f32[4,343,256]{2,1,0:T(8,128)S(1)} %reshape.48, f32[4,343,343]{2,0,1:T(4,128)S(1)} %copy-done), kind=kOutput, calls=%fused_computation.20 | convolution fusion | flops 1445670912 | bytes 4692240 | tf_op jit(solution)/shard_map/while/body/eval_jaxpr/cij,cjb->cib/dot_general | solution.py:36
  68.4 2.6 %reshape.102 = f32[1372,256]{1,0:T(8,128)} reshape(f32[4,343,256]{2,1,0:T(8,128)} %fusion.10) | data formatting | bytes 2809856 | tf_op jit(solution)/shard_map/while/body/eval_jaxpr/reshape | solution.py:39
  71.0 8.7 %scatter_custom_fusion.2 = f32[1008,256]{1,0:T(8,128)S(1)} fusion(s32[1372]{0:T(1024)S(1)} %fusion.28, f32[1372,256]{1,0:T(8,128)} %reshape.102, f32[]{:T(128)} %constant.34.clone.1), kind=kCustom, calls=%fused_computation.34 | custom fusion | flops 351232 | bytes 1032704 | tf_op jit(solution)/shard_map/while/body/eval_jaxpr/scatter-add | solution.py:39
  79.8 0.1 collective-permute-start.3
  79.8 1.0 slice.28
  80.8 0.0 copy-start.3
  80.8 6.4 %collective-permute-done.3 = f32[144,256]{1,0:T(8,128)S(1)} collective-permute-done((f32[144,256]{1,0:T(8,128)S(1)}, f32[144,256]{1,0:T(8,128)S(1)}, u32[]{:S(2)}, u32[]{:S(2)}) %collective-permute-start.3) | collective-permute-done | bytes 147488 | tf_op jit(solution)/shard_map/while/body/eval_jaxpr/ppermute | solution.py:26
  87.3 3.3 %scatter_fusion.1 = f32[864,256]{1,0:T(8,128)} fusion(f32[864,256]{1,0:T(8,128)} %slice.28, s32[144]{0:T(256)S(1)} %compare_select_fusion.1, f32[144,256]{1,0:T(8,128)S(1)} %collective-permute-done.3), kind=kCustom, calls=%fused_computation.7 | custom fusion | flops 36864 | bytes 442944 | tf_op jit(solution)/shard_map/while/body/eval_jaxpr/scatter-add | solution.py:45
  90.6 0.0 copy-done.3
  90.6 2.6 %multiply_subtract_fusion = f32[864,256]{1,0:T(8,128)} fusion(f32[864,256]{1,0:T(8,128)} %param.4, f32[864,256]{1,0:T(8,128)} %scatter_fusion.1, f32[864,256]{1,0:T(8,128)S(1)} %copy-done.3), kind=kLoop, calls=%fused_computation.24 | loop fusion | flops 1105920 | bytes 3538944 | tf_op jit(solution)/shard_map/while/body/eval_jaxpr/sub | solution.py:51
  93.2 1.5 collective-permute-start.4
  94.7 14.2 %collective-permute-done.4 = f32[864,256]{1,0:T(8,128)S(1)} collective-permute-done((f32[864,256]{1,0:T(8,128)}, f32[864,256]{1,0:T(8,128)S(1)}, u32[]{:S(2)}, u32[]{:S(2)}) %collective-permute-start.4) | collective-permute-done | bytes 884768 | tf_op jit(solution)/shard_map/ppermute | solution.py:16
  108.9 1.6 fusion.6
  110.5 0.0 copy-start.1
  110.5 1.2 copy-done.1
  111.7 4.5 %fusion.32 = f32[512,512]{1,0:T(8,128)} fusion(f32[864,512]{1,0:T(8,128)S(1)} %fusion.6), kind=kOutput, calls=%fused_computation.50 | convolution fusion | flops 2717908992 | bytes 2818048 | tf_op jit(solution)/shard_map/nb,nc->bc/dot_general | solution.py:56
  116.2 0.0 all-reduce.2.cloned.1.call-update
  116.2 96.2 %all-reduce.2.cloned.1.call-done = f32[512,512]{1,0:T(8,128)} async-done(((f32[512,512]{1,0:T(8,128)}), f32[512,512]{1,0:T(8,128)}) %all-reduce.2.cloned.1.call-update) | async-done | bytes 1048592 | tf_op jit(solution)/shard_map/psum | solution.py:57
  212.4 2.1 multiply_reduce_fusion
  215.2 4.1 %fusion.13 = f32[864,256]{1,0:T(8,128)} fusion(f32[864,512]{1,0:T(8,128)} %copy-done.1, f32[512,512]{1,0:T(8,128)} %all-reduce.2.cloned.1.call-done, s32[]{:T(128)S(6)} %select_n.42, f32[]{:T(128)S(6)} %sqrt.3), kind=kOutput, calls=%fused_computation.27 | convolution fusion | flops 1359872000 | bytes 3180032 | tf_op jit(solution)/shard_map/dot_general | solution.py:66
  (5 shorter events, 0.1 us)
Async XLA Ops:
  6.5 18.3 %copy-start = (f32[4,343,343]{2,0,1:T(4,128)S(1)}, f32[4,343,343]{2,0,1:T(4,128)}, u32[]{:S(2)}) copy-start(f32[4,343,343]{2,0,1:T(4,128)} %param.5) | copy-start | bytes 5647156
  6.5 205.9 %all-reduce.2.cloned.1.call-start = ((), (), s32[]{:S(2)}) async-start(), calls=%async_computation | async-start | bytes 2097152 | tf_op jit(solution)/shard_map/psum | solution.py:57
  9.3 8.2 %collective-permute-start = (f32[144,256]{1,0:T(8,128)S(1)}, f32[144,256]{1,0:T(8,128)S(1)}, u32[]{:S(2)}, u32[]{:S(2)}) collective-permute-start(f32[144,256]{1,0:T(8,128)S(1)} %gather_fusion), channel_id=1, source_target_pairs={{2,0},{4,2},{6,4},{8,6},{10,8},{12,10},{14,12},{16,14},{18,16},{20... | collective-permute-start | bytes 442376 | tf_op jit(solution)/shard_map/ppermute | solution.py:26
  39.9 1.0 copy-start.4
  40.8 7.4 %collective-permute-start.1 = (f32[144,256]{1,0:T(8,128)S(1)}, f32[144,256]{1,0:T(8,128)S(1)}, u32[]{:S(2)}, u32[]{:S(2)}) collective-permute-start(f32[144,256]{1,0:T(8,128)S(1)} %slice.27), channel_id=1, source_target_pairs={{30,0},{0,2},{2,4},{4,6},{6,8},{8,10},{10,12},{12,14},{14,16},{16,... | collective-permute-start | bytes 442376 | tf_op jit(solution)/shard_map/ppermute | solution.py:26
  50.0 4.5 %copy-start.2 = (f32[864,256]{1,0:T(8,128)}, f32[864,256]{1,0:T(8,128)S(1)}, u32[]{:S(2)}) copy-start(f32[864,256]{1,0:T(8,128)S(1)} %scatter_fusion) | copy-start | bytes 2654212
  54.5 2.9 %collective-permute-start.2 = (f32[144,256]{1,0:T(8,128)S(1)}, f32[144,256]{1,0:T(8,128)S(1)}, u32[]{:S(2)}, u32[]{:S(2)}) collective-permute-start(f32[144,256]{1,0:T(8,128)S(1)} %gather_fusion.2), channel_id=1, source_target_pairs={{2,0},{4,2},{6,4},{8,6},{10,8},{12,10},{14,12},{16,14},{18,16},{20... | collective-permute-start | bytes 442376 | tf_op jit(solution)/shard_map/while/body/eval_jaxpr/ppermute | solution.py:26
  79.8 7.5 %collective-permute-start.3 = (f32[144,256]{1,0:T(8,128)S(1)}, f32[144,256]{1,0:T(8,128)S(1)}, u32[]{:S(2)}, u32[]{:S(2)}) collective-permute-start(f32[144,256]{1,0:T(8,128)S(1)} %slice.29), channel_id=1, source_target_pairs={{30,0},{0,2},{2,4},{4,6},{6,8},{8,10},{10,12},{12,14},{14,16},{16,... | collective-permute-start | bytes 442376 | tf_op jit(solution)/shard_map/while/body/eval_jaxpr/ppermute | solution.py:26
  80.8 9.8 %copy-start.3 = (f32[864,256]{1,0:T(8,128)S(1)}, f32[864,256]{1,0:T(8,128)}, u32[]{:S(2)}) copy-start(f32[864,256]{1,0:T(8,128)} %copy-done.2) | copy-start | bytes 2654212
  93.2 15.7 %collective-permute-start.4 = (f32[864,256]{1,0:T(8,128)}, f32[864,256]{1,0:T(8,128)S(1)}, u32[]{:S(2)}, u32[]{:S(2)}) collective-permute-start(f32[864,256]{1,0:T(8,128)} %multiply_subtract_fusion), channel_id=1, source_target_pairs={{0,1},{1,0},{2,3},{3,2},{4,5},{5,4},{6,7},{7,6},{8,9},{9,8},{10,11... | collective-permute-start | bytes 2654216 | tf_op jit(solution)/shard_map/ppermute | solution.py:16
  110.5 1.2 copy-start.1
Sparse Core Ops, SparseCore 0:
  116.3 96.0 all-reduce.1
